TPU v7x, 32 devices: a whole 2x2x4 slice. The times are simulated.
32 devices in a mesh: grp: 2 (over y), win: 4 (over z), uly: 4 (over x, core).
Axes of the slice: x: 2, y: 2, z: 4, core: 2. Of those that a mesh axis runs over, the one named last changes fastest.
Arguments:
- query_rows: bfloat16 [8, 16, 64, 5120], P(('grp', 'win'), None, 'uly'), parts along dimension 0, may hold values from -140 to 140
- key_rows: bfloat16 [8, 16, 64, 5120], P(('grp', 'win'), None, 'uly'), parts along dimension 0, may hold values from -140 to 140
- value_rows: bfloat16 [8, 16, 64, 5120], P(('grp', 'win'), None, 'uly'), parts along dimension 0, may hold values from -6 to 6
- query_gain: float32 [5120], replicated, may hold values from 0.25 to 1.75
- key_gain: float32 [5120], replicated, may hold values from 0.25 to 1.75
- window_start: int32 [8], P('grp'), parts along dimension 0, may hold values from 0 to 40, as said below
- owner_of_phase: int32 [8], P('grp'), parts along dimension 0, may hold values from 0 to 3, each once
- blend_weight: int32 [8, 16], P('grp'), parts along dimension 0, may hold values from 1 to 8
Outputs:
- owned_frames: bfloat16 [96, 64, 5120], P(('grp', 'win'), 'uly'), parts along dimension 0
- next_windows: bfloat16 [8, 16, 64, 5120], P(('grp', 'win'), None, 'uly'), parts along dimension 0
There are 2 independent parts, one for each index of `grp`. A program takes and returns all parts, laid end to end along the dimension named above; an argument that names none is the same for every part. Nothing has to cross between parts.
Inputs may be any that keep to these rules, and one draw needn't show every extreme that they name: `window_start`: window w starts at frame w * 12 plus an offset of 0 to 4; in some pair of consecutive windows (the last one followed by the first counts as consecutive) the first offset is 4 and the second 0. `owner_of_phase`: a permutation.
All inputs are finite; a program needn't handle non-finite values.
Results may differ from a plain program's by a relative error of at most 0.0015.
The roundings to bfloat16 on the way count: a program that leaves them out, or rounds other values in their place, can miss the bound.
Values may be sent and summed in bfloat16 or wider, within the bound.
A program may use at most 128 MiB of HBM per device.

v0:
```python
import functools
import math

import jax
import jax.numpy as jnp
from jax import lax
from jax.experimental import pallas as pl
from jax.experimental.pallas import tpu as pltpu
from jax.sharding import PartitionSpec as P

HEADS = 40
WF = 16
FR = 12
VALUES_AHEAD = 2
CHUNKS = 4
LAG_BLEND = 1
LAG_RETURN = 2
LAG_LAST = 3
ROWS = 16


def fused(
    dims,
    start_ref,
    owner_ref,
    weight_ref,
    q_ref,
    k_ref,
    v_ref,
    qg_ref,
    kg_ref,
    owned_ref,
    next_ref,
    q_now,
    k_now,
    next_out,
    root,
    stage,
    inbox,
    vbox,
    attended,
    z_out,
    z_in,
    x_out,
    x_in,
    r_out,
    r_in,
    z_now,
    x_now,
    inverse,
    send_pos,
    first_at,
    second_at,
    first_w,
    second_w,
    target_slot,
    next_at,
    q_send,
    q_recv,
    k_send,
    k_recv,
    v_send,
    v_recv,
    zo_send,
    zo_recv,
    xo_send,
    xo_recv,
    ro_send,
    ro_recv,
    own_sem,
    next_sem,
    q_load,
    k_load,
):
    ulysses, windows, capacity, steps, head, tokens = dims
    local = tokens // WF
    me = lax.axis_index("uly")
    my_window = lax.axis_index("win")

    def peer(d):
        return lax.rem(me + d, ulysses)

    def far(d):
        return lax.rem(my_window + d, windows)

    chunk = tokens // CHUNKS

    def load(ref, now, sem, c):
        rows = pl.ds(pl.multiple_of(c * chunk, chunk), chunk)
        return pltpu.make_async_copy(ref.at[rows], now.at[rows], sem.at[c])

    for ref, now, sem in ((q_ref, q_now, q_load), (k_ref, k_now, k_load)):
        for c in range(CHUNKS):
            load(ref, now, sem, c).start()

    barrier = pltpu.get_barrier_semaphore()
    for d in range(1, ulysses):
        pl.semaphore_signal(
            barrier, inc=1, device_id={"uly": peer(d)}, device_id_type=pl.DeviceIdType.MESH
        )
    for d in range(1, windows):
        pl.semaphore_signal(
            barrier, inc=1, device_id={"win": far(d)}, device_id_type=pl.DeviceIdType.MESH
        )
    pl.semaphore_wait(barrier, ulysses + windows - 2)

    def spread(source, target, send, recv, axis):
        mine = me if axis == "uly" else my_window
        count = ulysses if axis == "uly" else windows
        for d in range(1, count):
            to = lax.rem(mine + d, count)
            pltpu.make_async_remote_copy(
                src_ref=source(to),
                dst_ref=target(mine),
                send_sem=send,
                recv_sem=recv,
                device_id={axis: to},
                device_id_type=pl.DeviceIdType.MESH,
            ).start()
        pltpu.make_async_copy(source(mine), target(mine), recv).start()

    def arrived(ref, sem):
        pltpu.make_async_copy(ref, ref, sem).wait()

    def columns(u, s):
        return pl.ds(pl.multiple_of((u * steps + s) * head, head), head)

    def scale_columns(which, s):
        now, gain = ((q_now, qg_ref), (k_now, kg_ref))[which]
        for u in range(ulysses):
            at = columns(u, s)
            scaled = now[:, at].astype(jnp.float32) * root[which] * gain[:, at]
            stage[which, u, s] = scaled.astype(jnp.bfloat16)

    def send_values(s):
        spread(
            lambda u: v_ref.at[:, columns(u, s)],
            lambda u: vbox.at[s, u],
            v_send.at[s],
            v_recv.at[s],
            "uly",
        )

    def send_scored(which, s):
        spread(
            lambda u: stage.at[which, u, s],
            lambda u: inbox.at[which, s, u],
            (q_send, k_send)[which].at[s],
            (q_recv, k_recv)[which].at[s],
            "uly",
        )

    for s in range(VALUES_AHEAD):
        send_values(s)

    frames_total = FR * windows
    shift = FR // 2

    def tables():
        my_start = start_ref[my_window]

        def invert(o, carry):
            def seek(phase, found):
                return jnp.where(owner_ref[phase] == o, phase, found)

            inverse[o] = lax.fori_loop(0, windows, seek, jnp.int32(0))
            return carry

        lax.fori_loop(0, windows, invert, 0)
        my_phase = inverse[my_window]

        def per_window(o, carry):
            for c in range(capacity):
                ahead = lax.rem(inverse[o] - my_start + frames_total, windows) + c * windows
                send_pos[o * capacity + c] = jnp.minimum(ahead, WF - 1)
                base = start_ref[o] + shift
                wanted = lax.rem(my_phase - base + 2 * frames_total, windows) + c * windows
                target_slot[o * capacity + c] = lax.rem(base + wanted, frames_total) // windows
            return carry

        lax.fori_loop(0, windows, per_window, 0)

        for f in range(FR):
            frame = f * windows + my_phase
            home = frame // FR
            before = lax.rem(home + windows - 1, windows)
            weight, place = [], []
            for w in (home, before):
                offset = lax.rem(frame - start_ref[w] + frames_total, frames_total)
                held = jnp.minimum(offset, WF - 1)
                weight.append(jnp.where(offset < WF, weight_ref[w, held], 0).astype(jnp.float32))
                place.append(w * capacity + held // windows)
            first_w[f], second_w[f] = weight
            first_at[f], second_at[f] = place
        for j in range(WF):
            needed = lax.rem(my_start + shift + j, windows)
            next_at[j] = owner_ref[needed] * capacity + j // windows

    for which, (ref, now, sem, gain) in enumerate(
        ((q_ref, q_now, q_load, qg_ref), (k_ref, k_now, k_load, kg_ref))
    ):

        def norm_block(t, carry, which=which, ref=ref, now=now, sem=sem, gain=gain):
            blocks = chunk // ROWS

            @pl.when(lax.rem(t, blocks) == 0)
            def _():
                load(ref, now, sem, t // blocks).wait()

            rows = pl.ds(pl.multiple_of(t * ROWS, ROWS), ROWS)
            floats = now[rows, :].astype(jnp.float32)
            mean_square = jnp.mean(floats * floats, axis=-1, keepdims=True)
            root[which, rows, :] = jnp.broadcast_to(
                lax.rsqrt(mean_square + 1e-06), (ROWS, head)
            )
            return carry

        lax.fori_loop(0, tokens // ROWS, norm_block, 0)
        scale_columns(which, 0)

    send_scored(0, 0)
    send_scored(1, 0)
    for which in range(2):
        scale_columns(which, 1)

    tables()

    scale = 1.0 / math.sqrt(head)

    def attention(s):
        arrived(inbox.at[0, s], q_recv.at[s])
        arrived(inbox.at[1, s], k_recv.at[s])
        arrived(vbox.at[s], v_recv.at[s])

        @pl.when(s + 1 < steps)
        def _():
            send_scored(0, s + 1)
            send_scored(1, s + 1)

        @pl.when(s + VALUES_AHEAD < steps)
        def _():
            send_values(s + VALUES_AHEAD)

        keys = inbox[1, s].reshape(ulysses * tokens, head)
        values = vbox[s].reshape(ulysses * tokens, head)
        for u in range(ulysses):
            scores = (
                lax.dot_general(
                    inbox[0, s, u],
                    keys,
                    (((1,), (1,)), ((), ())),
                    preferred_element_type=jnp.float32,
                )
                * scale
            )
            exponent = jnp.exp(scores - jnp.max(scores, axis=-1, keepdims=True))
            inverse_sum = 1.0 / jnp.sum(exponent, axis=-1, keepdims=True)
            weights = (exponent * inverse_sum).astype(jnp.bfloat16)
            result = jnp.dot(weights, values, preferred_element_type=jnp.float32)
            attended[:, u] = result.astype(jnp.bfloat16).reshape(WF, local, head)
        for o in range(windows):
            for c in range(capacity):
                z_out[s, o, c] = attended[send_pos[o * capacity + c]]
        spread(
            lambda o: z_out.at[s, o],
            lambda o: z_in.at[s, pl.ds(o * capacity, capacity)],
            zo_send.at[s],
            zo_recv.at[s],
            "win",
        )

        @pl.when(s + 2 < steps)
        def _():
            for which in range(2):
                scale_columns(which, s + 2)

    def blend(s):
        arrived(z_in.at[s], zo_recv.at[s])
        z_now[...] = z_in[s]
        for f in range(FR):
            numerator = first_w[f] * z_now[first_at[f]].astype(jnp.float32)
            numerator += second_w[f] * z_now[second_at[f]].astype(jnp.float32)
            x_out[s, :, f] = (numerator / (first_w[f] + second_w[f])).astype(jnp.bfloat16)
        spread(
            lambda u: x_out.at[s, u],
            lambda u: x_in.at[s, u],
            xo_send.at[s],
            xo_recv.at[s],
            "uly",
        )

    def give_back(s):
        arrived(x_in.at[s], xo_recv.at[s])
        x_now[...] = x_in[s]
        for o in range(windows):
            for c in range(capacity):
                r_out[s, o, c] = x_now[:, target_slot[o * capacity + c]]
        spread(
            lambda o: r_out.at[s, o],
            lambda o: r_in.at[s, pl.ds(o * capacity, capacity)],
            ro_send.at[s],
            ro_recv.at[s],
            "win",
        )
        for u in range(ulysses):
            pltpu.make_async_copy(
                x_in.at[s, u], owned_ref.at[:, :, columns(u, s)], own_sem.at[s]
            ).start()

    def finish(s):
        arrived(r_in.at[s], ro_recv.at[s])
        z_now[...] = r_in[s]
        for j in range(WF):
            next_out[s, :, j] = z_now[next_at[j]]
        for u in range(ulysses):
            pltpu.make_async_copy(
                next_out.at[s, u], next_ref.at[:, :, columns(u, s)], next_sem.at[s]
            ).start()

    def step(i, carry):
        for lag, work in (
            (0, attention),
            (LAG_RETURN, give_back),
            (LAG_BLEND, blend),
            (LAG_LAST, finish),
        ):

            @pl.when((i >= lag) & (i < steps + lag))
            def _(lag=lag, work=work):
                work(i - lag)

        return carry

    lax.fori_loop(0, steps + LAG_LAST, step, 0)

    def sent(s, carry):
        arrived(inbox.at[0, s, pl.ds(0, ulysses - 1)], q_send.at[s])
        arrived(inbox.at[1, s, pl.ds(0, ulysses - 1)], k_send.at[s])
        arrived(vbox.at[s, pl.ds(0, ulysses - 1)], v_send.at[s])
        arrived(z_out.at[s, pl.ds(0, windows - 1)], zo_send.at[s])
        arrived(x_out.at[s, pl.ds(0, ulysses - 1)], xo_send.at[s])
        arrived(r_out.at[s, pl.ds(0, windows - 1)], ro_send.at[s])
        arrived(x_in.at[s], own_sem.at[s])
        arrived(next_out.at[s], next_sem.at[s])
        return carry

    lax.fori_loop(0, steps, sent, 0)


def per_device(
    query_rows,
    key_rows,
    value_rows,
    query_gain,
    key_gain,
    window_start,
    owner_of_phase,
    blend_weight,
):
    windows = lax.axis_size("win")
    ulysses = lax.axis_size("uly")
    capacity = (WF + windows - 1) // windows
    local = query_rows.shape[2]
    features = query_rows.shape[3]
    head = features // HEADS
    steps = HEADS // ulysses
    tokens = WF * local
    smem = pl.BlockSpec(memory_space=pltpu.SMEM)
    vmem = pl.BlockSpec(memory_space=pltpu.VMEM)
    hbm = pl.BlockSpec(memory_space=pl.ANY)
    bf16 = jnp.bfloat16
    sems = pltpu.SemaphoreType.DMA((steps,))
    frame = (ulysses, local, head)
    owned, next_rows = pl.pallas_call(
        functools.partial(fused, (ulysses, windows, capacity, steps, head, tokens)),
        out_shape=(
            jax.ShapeDtypeStruct((FR, local, features), bf16),
            jax.ShapeDtypeStruct((WF, local, features), bf16),
        ),
        in_specs=[smem] * 3 + [hbm] * 3 + [vmem] * 2,
        out_specs=(hbm, hbm),
        scratch_shapes=[
            pltpu.VMEM((tokens, features), bf16),
            pltpu.VMEM((tokens, features), bf16),
            pltpu.VMEM((steps, ulysses, WF, local, head), bf16),
            pltpu.VMEM((2, tokens, head), jnp.float32),
            pltpu.VMEM((2, ulysses, steps, tokens, head), bf16),
            pltpu.VMEM((2, steps, ulysses, tokens, head), bf16),
            pltpu.VMEM((steps, ulysses, tokens, head), bf16),
            pltpu.VMEM((WF,) + frame, bf16),
            pltpu.VMEM((steps, windows, capacity) + frame, bf16),
            pltpu.VMEM((steps, windows * capacity) + frame, bf16),
            pltpu.VMEM((steps, ulysses, FR, local, head), bf16),
            pltpu.VMEM((steps, ulysses, FR, local, head), bf16),
            pltpu.VMEM((steps, windows, capacity) + frame, bf16),
            pltpu.VMEM((steps, windows * capacity) + frame, bf16),
            pltpu.VMEM((windows * capacity,) + frame, bf16),
            pltpu.VMEM((ulysses, FR, local, head), bf16),
            pltpu.SMEM((windows,), jnp.int32),
            pltpu.SMEM((windows * capacity,), jnp.int32),
            pltpu.SMEM((FR,), jnp.int32),
            pltpu.SMEM((FR,), jnp.int32),
            pltpu.SMEM((FR,), jnp.float32),
            pltpu.SMEM((FR,), jnp.float32),
            pltpu.SMEM((windows * capacity,), jnp.int32),
            pltpu.SMEM((WF,), jnp.int32),
        ]
        + [sems] * 14
        + [pltpu.SemaphoreType.DMA((CHUNKS,))] * 2,
        compiler_params=pltpu.CompilerParams(
            collective_id=0, has_side_effects=True, vmem_limit_bytes=66 * 1000 * 1000
        ),
    )(
        window_start,
        owner_of_phase,
        blend_weight,
        query_rows.reshape(tokens, features),
        key_rows.reshape(tokens, features),
        value_rows.reshape(tokens, features),
        query_gain.reshape(1, features),
        key_gain.reshape(1, features),
    )
    return (owned, next_rows[None])


def solution(mesh):
    placed = (
        P(("grp", "win"), None, "uly", None),
        P(("grp", "win"), None, "uly", None),
        P(("grp", "win"), None, "uly", None),
        P(),
        P(),
        P("grp"),
        P("grp"),
        P("grp", None),
    )
    return jax.shard_map(
        per_device,
        mesh=mesh,
        in_specs=placed,
        out_specs=(P(("grp", "win"), "uly", None), P(("grp", "win"), None, "uly", None)),
        check_vma=False,
    )
```

profile of v0, /device:TPU:0, one launch (start us, length us, event | category | flops | bytes accessed | tf_op | source)
XLA Modules:
  0.0 145.1 jit_solution(2237909567700092697)
XLA Ops:
  0.6 139.9 %shard_map.95 = (bf16[12,16,5120]{2,1,0:T(8,128)(2,1)}, bf16[16,16,5120]{2,1,0:T(8,128)(2,1)}) custom-call(s32[4]{0:T(128)} %start_ref.1, s32[4]{0:T(128)} %owner_ref.1, s32[4,16]{1,0:T(4,128)} %weight_ref.1, bf16[256,5120]{1,0:T(8,128)(2,1)} %bitcast.6, bf16[256,5120]{1,0:T(8,128)(2,1)} %bitcast.7, bf16[256,5120]{1,0:T(8,128)(2,1)} %bitcast.8, ...), custom_call_target="tpu_custom_call" | custom-call | tf_op jit(solution)/shard_map/pallas_call | solution.py:374
  140.5 0.0 copy-start
  140.5 3.1 %copy.12 = bf16[12,16,5120]{2,1,0:T(8,128)(2,1)} copy(bf16[12,16,5120]{2,1,0:T(8,128)(2,1)} %get-tuple-element.8) | data formatting | bytes 3932160
  143.6 0.0 copy-done
  143.6 1.5 %copy.13 = bf16[1,16,16,5120]{3,2,1,0:T(8,128)(2,1)} copy(bf16[1,16,16,5120]{3,2,1,0:T(8,128)(2,1)S(1)} %bitcast.9) | data formatting | bytes 5242880
Async XLA Ops:
  140.5 3.1 %copy-start = (bf16[16,16,5120]{2,1,0:T(8,128)(2,1)S(1)}, bf16[16,16,5120]{2,1,0:T(8,128)(2,1)}, u32[]{:S(2)}) copy-start(bf16[16,16,5120]{2,1,0:T(8,128)(2,1)} %get-tuple-element.5) | copy-start | bytes 7864324
where the time goes:
time: 145 us
  Pallas kernels  140 us (97%)
  local copies, waits for them, and re-layouts  4.59 us (3%)
    pallas_call x1, Pallas kernels, per_device(): pl.pallas_call(functools.partial(fused, (ulysses, windows, capacity, step...  140 us
    unnamed x4, local copies, waits for them, and re-layouts  4.59 us

commit v1 on v0

v1 whole, which is shorter than its diff:
```python
import functools
import math

import jax
import jax.numpy as jnp
from jax import lax
from jax.experimental import pallas as pl
from jax.experimental.pallas import tpu as pltpu
from jax.sharding import PartitionSpec as P

HEADS = 40
WF = 16
FR = 12
HALO = WF - FR
SHIFT = FR // 2
AHEAD = HALO + SHIFT
CHUNKS = 4
LAG_BLEND = 1
LAG_RETURN = 1
LAG_LAST = 2
ROWS = 16


def fused(
    dims,
    start_ref,
    owner_ref,
    weight_ref,
    q_ref,
    k_ref,
    v_ref,
    qg_ref,
    kg_ref,
    owned_ref,
    next_ref,
    q_now,
    k_now,
    root,
    stage,
    inbox,
    vbox,
    attended,
    halo_in,
    halo_now,
    x_out,
    x_in,
    r_out,
    r_in,
    n_in,
    pool,
    inverse,
    near_at,
    near_w,
    far_at,
    far_w,
    give_at,
    owned_at,
    q_send,
    q_recv,
    k_send,
    k_recv,
    v_send,
    v_recv,
    ho_send,
    ho_recv,
    xo_send,
    xo_recv,
    ro_send,
    ro_recv,
    no_send,
    no_recv,
    q_load,
    k_load,
):
    ulysses, windows, share, given, steps, head, tokens = dims
    local = tokens // WF
    me = lax.axis_index("uly")
    my_window = lax.axis_index("win")
    below = lax.rem(my_window + windows - 1, windows)
    above = lax.rem(my_window + 1, windows)

    def peer(d):
        return lax.rem(me + d, ulysses)

    def far(d):
        return lax.rem(my_window + d, windows)

    def given_slots(d):
        return (0, 1) if d == 1 else (1 + (d - 2) * share, share)

    chunk = tokens // CHUNKS

    def load(ref, now, sem, c):
        rows = pl.ds(pl.multiple_of(c * chunk, chunk), chunk)
        return pltpu.make_async_copy(ref.at[rows], now.at[rows], sem.at[c])

    for ref, now, sem in ((q_ref, q_now, q_load), (k_ref, k_now, k_load)):
        for c in range(CHUNKS):
            load(ref, now, sem, c).start()

    barrier = pltpu.get_barrier_semaphore()
    for d in range(1, ulysses):
        pl.semaphore_signal(
            barrier, inc=1, device_id={"uly": peer(d)}, device_id_type=pl.DeviceIdType.MESH
        )
    for d in range(1, windows):
        pl.semaphore_signal(
            barrier, inc=1, device_id={"win": far(d)}, device_id_type=pl.DeviceIdType.MESH
        )

    def remote(source, target, send, recv, axis, to):
        pltpu.make_async_remote_copy(
            src_ref=source,
            dst_ref=target,
            send_sem=send,
            recv_sem=recv,
            device_id={axis: to},
            device_id_type=pl.DeviceIdType.MESH,
        ).start()

    def spread(source, target, send, recv):
        for d in range(1, ulysses):
            to = peer(d)
            remote(source(to), target(me), send, recv, "uly", to)
        pltpu.make_async_copy(source(me), target(me), recv).start()

    def arrived(ref, sem):
        pltpu.make_async_copy(ref, ref, sem).wait()

    def columns(u, s):
        return pl.ds(pl.multiple_of((u * steps + s) * head, head), head)

    def scale_columns(which, s):
        now, gain = ((q_now, qg_ref), (k_now, kg_ref))[which]
        for u in range(ulysses):
            at = columns(u, s)
            scaled = now[:, at].astype(jnp.float32) * root[which] * gain[:, at]
            stage[which, u, s] = scaled.astype(jnp.bfloat16)

    def send_values(s):
        spread(
            lambda u: v_ref.at[:, columns(u, s)],
            lambda u: vbox.at[s, u],
            v_send.at[s],
            v_recv.at[s],
        )

    def send_scored(which, s):
        spread(
            lambda u: stage.at[which, u, s],
            lambda u: inbox.at[which, s, u],
            (q_send, k_send)[which].at[s],
            (q_recv, k_recv)[which].at[s],
        )

    frames_total = FR * windows

    def tables():
        def invert(o, carry):
            def seek(phase, found):
                return jnp.where(owner_ref[phase] == o, phase, found)

            inverse[o] = lax.fori_loop(0, windows, seek, jnp.int32(0))
            return carry

        lax.fori_loop(0, windows, invert, 0)
        my_phase = inverse[my_window]
        first = FR * my_window + HALO

        def per_owner(o, carry):
            rest = lax.rem(inverse[o] - first + frames_total, windows)
            for c in range(share):
                give_at[o * share + c] = jnp.minimum(rest + c * windows, FR - 1)
            return carry

        lax.fori_loop(0, windows, per_owner, 0)
        rest = lax.rem(inverse[below] - first + frames_total, windows)
        extra = jnp.int32(AHEAD)
        for f in range(AHEAD, FR):
            extra = jnp.where(rest == f % windows, f, extra)
        give_at[below * share] = extra


        def offset_of(w):
            return jnp.clip(start_ref[w] - FR * w, 0, HALO)

        offset = offset_of(my_window)
        offset_below = offset_of(below)
        offset_above = offset_of(above)
        for f in range(FR):
            own = f + HALO - offset
            near_at[f] = own
            near_w[f] = weight_ref[my_window, own].astype(jnp.float32)
            if f < HALO:
                at = f + WF - offset_below
                held = at < WF
                at = jnp.minimum(at, WF - 1)
                far_at[f] = at - FR
                far_w[f] = jnp.where(held, weight_ref[below, at], 0).astype(jnp.float32)
            elif f >= FR - HALO:
                at = f - (FR - HALO) - offset_above
                held = at >= 0
                at = jnp.maximum(at, 0)
                far_at[f] = at + HALO
                far_w[f] = jnp.where(held, weight_ref[above, at], 0).astype(jnp.float32)
        for f in range(FR):
            place = lax.rem(f * windows + my_phase - HALO + frames_total, frames_total)
            home = place // FR
            at = place - home * FR
            apart = lax.rem(home - my_window + windows, windows)
            given_at = FR + AHEAD + 1 + (apart - 2) * share + at // windows
            ahead = FR + jnp.minimum(at, AHEAD)
            owned_at[f] = jnp.where(
                home == my_window, at, jnp.where(home == above, ahead, given_at)
            )
        return offset + SHIFT - HALO

    for which, (ref, now, sem, gain) in enumerate(
        ((q_ref, q_now, q_load, qg_ref), (k_ref, k_now, k_load, kg_ref))
    ):

        def norm_block(t, carry, which=which, ref=ref, now=now, sem=sem, gain=gain):
            blocks = chunk // ROWS

            @pl.when(lax.rem(t, blocks) == 0)
            def _():
                load(ref, now, sem, t // blocks).wait()

            rows = pl.ds(pl.multiple_of(t * ROWS, ROWS), ROWS)
            floats = now[rows, :].astype(jnp.float32)
            mean_square = jnp.mean(floats * floats, axis=-1, keepdims=True)
            root[which, rows, :] = jnp.broadcast_to(
                lax.rsqrt(mean_square + 1e-06), (ROWS, head)
            )
            return carry

        lax.fori_loop(0, tokens // ROWS, norm_block, 0)
        scale_columns(which, 0)

    pl.semaphore_wait(barrier, ulysses + windows - 2)

    send_scored(0, 0)
    send_scored(1, 0)
    send_values(0)
    for which in range(2):
        scale_columns(which, 1)
    send_values(1)

    next_at = tables()

    scale = 1.0 / math.sqrt(head)

    def attention(s):
        arrived(inbox.at[0, s], q_recv.at[s])
        arrived(inbox.at[1, s], k_recv.at[s])
        arrived(vbox.at[s], v_recv.at[s])

        @pl.when(s + 1 < steps)
        def _():
            send_scored(0, s + 1)
            send_scored(1, s + 1)

        @pl.when(s + 2 < steps)
        def _():
            send_values(s + 2)

        keys = inbox[1, s].reshape(ulysses * tokens, head)
        values = vbox[s].reshape(ulysses * tokens, head)
        for u in range(ulysses):
            scores = (
                lax.dot_general(
                    inbox[0, s, u],
                    keys,
                    (((1,), (1,)), ((), ())),
                    preferred_element_type=jnp.float32,
                )
                * scale
            )
            exponent = jnp.exp(scores - jnp.max(scores, axis=-1, keepdims=True))
            inverse_sum = 1.0 / jnp.sum(exponent, axis=-1, keepdims=True)
            weights = (exponent * inverse_sum).astype(jnp.bfloat16)
            result = jnp.dot(weights, values, preferred_element_type=jnp.float32)
            attended[s, :, u] = result.astype(jnp.bfloat16).reshape(WF, local, head)
        remote(
            attended.at[s, pl.ds(0, HALO)],
            halo_in.at[s, 1],
            ho_send.at[s],
            ho_recv.at[s],
            "win",
            below,
        )
        remote(
            attended.at[s, pl.ds(FR, HALO)],
            halo_in.at[s, 0],
            ho_send.at[s],
            ho_recv.at[s],
            "win",
            above,
        )

        @pl.when(s + 2 < steps)
        def _():
            for which in range(2):
                scale_columns(which, s + 2)

    def blend(s):
        arrived(halo_in.at[s], ho_recv.at[s])
        for side in range(2):
            halo_now[side * HALO : (side + 1) * HALO] = halo_in[s, side]
        for f in range(FR):
            numerator = near_w[f] * attended[s, near_at[f]].astype(jnp.float32)
            denominator = near_w[f]
            if f < HALO or f >= FR - HALO:
                numerator += far_w[f] * halo_now[far_at[f]].astype(jnp.float32)
                denominator += far_w[f]
            x_out[s, :, f] = (numerator / denominator).astype(jnp.bfloat16)
        spread(
            lambda u: x_out.at[s, u],
            lambda u: x_in.at[s, u],
            xo_send.at[s],
            xo_recv.at[s],
        )

    def give_back(s):
        arrived(x_in.at[s], xo_recv.at[s])
        remote(
            x_in.at[s, :, pl.ds(0, AHEAD)],
            n_in.at[s],
            no_send.at[s],
            no_recv.at[s],
            "win",
            below,
        )
        for f in range(FR):
            pool[f] = x_in[s, :, f]
        for d in range(1, windows):
            o = far(d)
            base, count = given_slots(windows - d)
            for c in range(count):
                r_out[s, base + c] = pool[give_at[o * share + c]]
            many = pl.ds(base, count)
            remote(
                r_out.at[s, many], r_in.at[s, many], ro_send.at[s], ro_recv.at[s], "win", o
            )

    def finish(s):
        arrived(n_in.at[s], no_recv.at[s])
        arrived(r_in.at[s], ro_recv.at[s])
        for f in range(FR):
            pool[f] = x_in[s, :, f]
        for f in range(AHEAD):
            pool[FR + f] = n_in[s, :, f]
        for c in range(given):
            pool[FR + AHEAD + c] = r_in[s, c]
        for f in range(FR):
            frame = pool[owned_at[f]]
            for u in range(ulysses):
                owned_ref[f, :, columns(u, s)] = frame[u]
        for j in range(WF):
            frame = pool[next_at + j]
            for u in range(ulysses):
                next_ref[j, :, columns(u, s)] = frame[u]

    def step(i, carry):
        for lag, work in (
            (LAG_BLEND, blend),
            (0, attention),
            (LAG_RETURN, give_back),
            (LAG_LAST, finish),
        ):

            @pl.when((i >= lag) & (i < steps + lag))
            def _(lag=lag, work=work):
                work(i - lag)

        return carry

    lax.fori_loop(0, steps + LAG_LAST, step, 0)

    def sent(s, carry):
        arrived(inbox.at[0, s, pl.ds(0, ulysses - 1)], q_send.at[s])
        arrived(inbox.at[1, s, pl.ds(0, ulysses - 1)], k_send.at[s])
        arrived(vbox.at[s, pl.ds(0, ulysses - 1)], v_send.at[s])
        arrived(halo_in.at[s], ho_send.at[s])
        arrived(x_out.at[s, pl.ds(0, ulysses - 1)], xo_send.at[s])
        arrived(n_in.at[s], no_send.at[s])
        arrived(r_in.at[s], ro_send.at[s])
        return carry

    lax.fori_loop(0, steps, sent, 0)


def per_device(
    query_rows,
    key_rows,
    value_rows,
    query_gain,
    key_gain,
    window_start,
    owner_of_phase,
    blend_weight,
):
    windows = lax.axis_size("win")
    ulysses = lax.axis_size("uly")
    share = (FR + windows - 1) // windows
    given = 1 + (windows - 2) * share
    local = query_rows.shape[2]
    features = query_rows.shape[3]
    head = features // HEADS
    steps = HEADS // ulysses
    tokens = WF * local
    smem = pl.BlockSpec(memory_space=pltpu.SMEM)
    vmem = pl.BlockSpec(memory_space=pltpu.VMEM)
    hbm = pl.BlockSpec(memory_space=pl.ANY)
    bf16 = jnp.bfloat16
    sems = pltpu.SemaphoreType.DMA((steps,))
    frame = (ulysses, local, head)
    owned, next_rows = pl.pallas_call(
        functools.partial(fused, (ulysses, windows, share, given, steps, head, tokens)),
        out_shape=(
            pltpu.VMEM((FR, local, features), bf16),
            pltpu.VMEM((WF, local, features), bf16),
        ),
        in_specs=[smem] * 3 + [hbm] * 3 + [vmem] * 2,
        out_specs=(vmem, vmem),
        scratch_shapes=[
            pltpu.VMEM((tokens, features), bf16),
            pltpu.VMEM((tokens, features), bf16),
            pltpu.VMEM((2, tokens, head), jnp.float32),
            pltpu.VMEM((2, ulysses, steps, tokens, head), bf16),
            pltpu.VMEM((2, steps, ulysses, tokens, head), bf16),
            pltpu.VMEM((steps, ulysses, tokens, head), bf16),
            pltpu.VMEM((steps, WF) + frame, bf16),
            pltpu.VMEM((steps, 2, HALO) + frame, bf16),
            pltpu.VMEM((2 * HALO,) + frame, bf16),
            pltpu.VMEM((steps, ulysses, FR, local, head), bf16),
            pltpu.VMEM((steps, ulysses, FR, local, head), bf16),
            pltpu.VMEM((steps, given) + frame, bf16),
            pltpu.VMEM((steps, given) + frame, bf16),
            pltpu.VMEM((steps, ulysses, AHEAD, local, head), bf16),
            pltpu.VMEM((FR + AHEAD + given,) + frame, bf16),
            pltpu.SMEM((windows,), jnp.int32),
            pltpu.SMEM((FR,), jnp.int32),
            pltpu.SMEM((FR,), jnp.float32),
            pltpu.SMEM((FR,), jnp.int32),
            pltpu.SMEM((FR,), jnp.float32),
            pltpu.SMEM((windows * share,), jnp.int32),
            pltpu.SMEM((FR,), jnp.int32),
        ]
        + [sems] * 14
        + [pltpu.SemaphoreType.DMA((CHUNKS,))] * 2,
        compiler_params=pltpu.CompilerParams(
            collective_id=0, has_side_effects=True, vmem_limit_bytes=62 * 1000 * 1000
        ),
    )(
        window_start,
        owner_of_phase,
        blend_weight,
        query_rows.reshape(tokens, features),
        key_rows.reshape(tokens, features),
        value_rows.reshape(tokens, features),
        query_gain.reshape(1, features),
        key_gain.reshape(1, features),
    )
    return (owned, next_rows[None])


def solution(mesh):
    placed = (
        P(("grp", "win"), None, "uly", None),
        P(("grp", "win"), None, "uly", None),
        P(("grp", "win"), None, "uly", None),
        P(),
        P(),
        P("grp"),
        P("grp"),
        P("grp", None),
    )
    return jax.shard_map(
        per_device,
        mesh=mesh,
        in_specs=placed,
        out_specs=(P(("grp", "win"), "uly", None), P(("grp", "win"), None, "uly", None)),
        check_vma=False,
    )
```

time: 145 us -> 139 us (0.959)
  Pallas kernels: 140 us -> 135 us
  local copies, waits for them, and re-layouts: 4.59 us -> 2.77 us
    pallas_call x1, Pallas kernels: 140 us -> 135 us  [per_device(): pl.pallas_call(functools.partial(fused, (ulysses, windows, share, given,...]
    unnamed x4 -> x2, local copies, waits for them, and re-layouts: 4.59 us -> 2.77 us
where the time goes in v1:
time: 139 us; the launch traced here: 138 us
  Pallas kernels  135 us (97%)
  local copies, waits for them, and re-layouts  2.77 us (2%)
    pallas_call x1, Pallas kernels, per_device(): pl.pallas_call(functools.partial(fused, (ulysses, windows, share, given,...  135 us

profile of v1, /device:TPU:0, one launch (start us, length us, event | category | flops | bytes accessed | tf_op | source)
XLA Modules:
  0.0 138.4 jit_solution(12924163834933520053)
XLA Ops:
  0.6 134.9 %shard_map.95 = (bf16[12,16,5120]{2,1,0:T(8,128)(2,1)S(1)}, bf16[16,16,5120]{2,1,0:T(8,128)(2,1)S(1)}) custom-call(s32[4]{0:T(128)} %start_ref.1, s32[4]{0:T(128)} %owner_ref.1, s32[4,16]{1,0:T(4,128)} %weight_ref.1, bf16[256,5120]{1,0:T(8,128)(2,1)} %bitcast.7, bf16[256,5120]{1,0:T(8,128)(2,1)} %bitcast.8, bf16[256,5120]{1,0:T(8,128)(2,1)} %bitcast.9, ...), custom_call_target="tpu_custom_call" | custom-call | tf_op jit(solution)/shard_map/pallas_call | solution.py:418
  135.6 1.3 copy.12
  136.9 1.5 %copy.13 = bf16[1,16,16,5120]{3,2,1,0:T(8,128)(2,1)} copy(bf16[1,16,16,5120]{3,2,1,0:T(8,128)(2,1)S(1)} %bitcast.6) | data formatting | bytes 5242880

commit v2 on v1

--- a/solution.py
+++ b/solution.py
@@ -48,6 +48,11 @@
     r_in,
     n_in,
     pool,
+    raw_out,
+    raw_in,
+    blended,
+    rl_out,
+    rl_in,
     inverse,
     near_at,
     near_w,
@@ -69,6 +74,10 @@
     ro_recv,
     no_send,
     no_recv,
+    raw_send,
+    raw_recv,
+    n_last,
+    r_last,
     q_load,
     k_load,
 ):
@@ -85,6 +94,12 @@
     def far(d):
         return lax.rem(my_window + d, windows)
 
+    def near_first(d):
+        if ulysses % 2:
+            return peer(d)
+        pair = lax.rem(lax.div(me, 2) + d // 2, ulysses // 2)
+        return pair * 2 + lax.rem(me + d, 2)
+
     def given_slots(d):
         return (0, 1) if d == 1 else (1 + (d - 2) * share, share)
 
@@ -108,20 +123,20 @@
             barrier, inc=1, device_id={"win": far(d)}, device_id_type=pl.DeviceIdType.MESH
         )
 
-    def remote(source, target, send, recv, axis, to):
+    def remote(source, target, send, recv, to):
         pltpu.make_async_remote_copy(
             src_ref=source,
             dst_ref=target,
             send_sem=send,
             recv_sem=recv,
-            device_id={axis: to},
+            device_id=to,
             device_id_type=pl.DeviceIdType.MESH,
         ).start()
 
     def spread(source, target, send, recv):
         for d in range(1, ulysses):
-            to = peer(d)
-            remote(source(to), target(me), send, recv, "uly", to)
+            to = near_first(d)
+            remote(source(to), target(me), send, recv, {"uly": to})
         pltpu.make_async_copy(source(me), target(me), recv).start()
 
     def arrived(ref, sem):
@@ -150,7 +165,7 @@
             lambda u: stage.at[which, u, s],
             lambda u: inbox.at[which, s, u],
             (q_send, k_send)[which].at[s],
-            (q_recv, k_recv)[which].at[s],
+            q_recv.at[s, me] if which == 0 else k_recv.at[s],
         )
 
     frames_total = FR * windows
@@ -239,34 +254,22 @@
 
     pl.semaphore_wait(barrier, ulysses + windows - 2)
 
-    send_scored(0, 0)
     send_scored(1, 0)
     send_values(0)
+    send_scored(0, 0)
     for which in range(2):
         scale_columns(which, 1)
-    send_values(1)
 
     next_at = tables()
 
     scale = 1.0 / math.sqrt(head)
 
-    def attention(s):
-        arrived(inbox.at[0, s], q_recv.at[s])
-        arrived(inbox.at[1, s], k_recv.at[s])
-        arrived(vbox.at[s], v_recv.at[s])
-
-        @pl.when(s + 1 < steps)
-        def _():
-            send_scored(0, s + 1)
-            send_scored(1, s + 1)
-
-        @pl.when(s + 2 < steps)
-        def _():
-            send_values(s + 2)
-
+    def attend(s, then):
         keys = inbox[1, s].reshape(ulysses * tokens, head)
         values = vbox[s].reshape(ulysses * tokens, head)
-        for u in range(ulysses):
+        for d in range(ulysses):
+            u = near_first(d)
+            arrived(inbox.at[0, s, u], q_recv.at[s, u])
             scores = (
                 lax.dot_general(
                     inbox[0, s, u],
@@ -280,23 +283,35 @@
             inverse_sum = 1.0 / jnp.sum(exponent, axis=-1, keepdims=True)
             weights = (exponent * inverse_sum).astype(jnp.bfloat16)
             result = jnp.dot(weights, values, preferred_element_type=jnp.float32)
-            attended[s, :, u] = result.astype(jnp.bfloat16).reshape(WF, local, head)
-        remote(
-            attended.at[s, pl.ds(0, HALO)],
-            halo_in.at[s, 1],
-            ho_send.at[s],
-            ho_recv.at[s],
-            "win",
-            below,
-        )
-        remote(
-            attended.at[s, pl.ds(FR, HALO)],
-            halo_in.at[s, 0],
-            ho_send.at[s],
-            ho_recv.at[s],
-            "win",
-            above,
-        )
+            then(u, result.astype(jnp.bfloat16).reshape(WF, local, head))
+
+    def both_halos(halo_below, halo_above):
+        pl.when(my_window > 0)(halo_below)
+        halo_above()
+        pl.when(my_window == 0)(halo_below)
+
+    def attention(s):
+        arrived(inbox.at[1, s], k_recv.at[s])
+        arrived(vbox.at[s], v_recv.at[s])
+        send_scored(1, s + 1)
+        send_values(s + 1)
+        send_scored(0, s + 1)
+
+        def keep(u, result):
+            attended[s, :, u] = result
+
+        attend(s, keep)
+
+        def send(side, at, to):
+            return lambda: remote(
+                attended.at[s, pl.ds(at, HALO)],
+                halo_in.at[s, side],
+                ho_send.at[s],
+                ho_recv.at[s],
+                {"win": to},
+            )
+
+        both_halos(send(1, 0, below), send(0, FR, above))
 
         @pl.when(s + 2 < steps)
         def _():
@@ -321,27 +336,40 @@
             xo_recv.at[s],
         )
 
+    def to_all(give):
+        for d in range(1, windows):
+
+            @pl.when(my_window + d < windows)
+            def _(d=d):
+                give(my_window + d, windows - d)
+
+            @pl.when(my_window >= d)
+            def _(d=d):
+                give(my_window - d, d)
+
     def give_back(s):
         arrived(x_in.at[s], xo_recv.at[s])
-        remote(
-            x_in.at[s, :, pl.ds(0, AHEAD)],
-            n_in.at[s],
-            no_send.at[s],
-            no_recv.at[s],
-            "win",
-            below,
-        )
         for f in range(FR):
             pool[f] = x_in[s, :, f]
-        for d in range(1, windows):
-            o = far(d)
-            base, count = given_slots(windows - d)
+
+        def give(o, apart):
+            base, count = given_slots(apart)
             for c in range(count):
                 r_out[s, base + c] = pool[give_at[o * share + c]]
             many = pl.ds(base, count)
             remote(
-                r_out.at[s, many], r_in.at[s, many], ro_send.at[s], ro_recv.at[s], "win", o
+                r_out.at[s, many], r_in.at[s, many], ro_send.at[s], ro_recv.at[s], {"win": o}
             )
+            if apart == 1:
+                remote(
+                    x_in.at[s, :, pl.ds(0, AHEAD)],
+                    n_in.at[s],
+                    no_send.at[s],
+                    no_recv.at[s],
+                    {"win": o},
+                )
+
+        to_all(give)
 
     def finish(s):
         arrived(n_in.at[s], no_recv.at[s])
@@ -361,6 +389,93 @@
             for u in range(ulysses):
                 next_ref[j, :, columns(u, s)] = frame[u]
 
+    last = steps - 1
+
+    def last_attention():
+        arrived(inbox.at[1, last], k_recv.at[last])
+        arrived(vbox.at[last], v_recv.at[last])
+
+        def give_raw(u, result):
+            raw_out[u] = result
+
+            def send(side, at, to):
+                return lambda: remote(
+                    raw_out.at[u, pl.ds(at, HALO)],
+                    raw_in.at[me, pl.ds(FR + side * HALO, HALO)],
+                    raw_send.at[u],
+                    raw_recv.at[me],
+                    {"win": to, "uly": u},
+                )
+
+            both_halos(send(1, 0, below), send(0, FR, above))
+            for f in range(FR):
+                x_out[last, u, f] = raw_out[u, near_at[f]]
+            home = raw_in.at[me, pl.ds(0, FR)]
+
+            @pl.when(u != me)
+            def _():
+                remote(x_out.at[last, u], home, xo_send.at[last], raw_recv.at[me], {"uly": u})
+
+            @pl.when(u == me)
+            def _():
+                pltpu.make_async_copy(x_out.at[last, u], home, raw_recv.at[me]).start()
+
+        attend(last, give_raw)
+
+    def last_blend():
+        for d in range(ulysses):
+            m = near_first(d)
+            arrived(raw_in.at[m], raw_recv.at[m])
+            for f in range(2 * HALO):
+                halo_now[f, 0] = raw_in[m, FR + f]
+            for f in range(FR):
+                numerator = near_w[f] * raw_in[m, f].astype(jnp.float32)
+                denominator = near_w[f]
+                if f < HALO or f >= FR - HALO:
+                    numerator += far_w[f] * halo_now[far_at[f], 0].astype(jnp.float32)
+                    denominator += far_w[f]
+                blended[m, f] = (numerator / denominator).astype(jnp.bfloat16)
+
+            def give(o, apart):
+                base, count = given_slots(apart)
+                for c in range(count):
+                    rl_out[m, base + c] = blended[m, give_at[o * share + c]]
+                many = pl.ds(base, count)
+                remote(
+                    rl_out.at[m, many],
+                    rl_in.at[m, many],
+                    ro_send.at[last],
+                    r_last.at[m],
+                    {"win": o},
+                )
+                if apart == 1:
+                    remote(
+                        blended.at[m, pl.ds(0, AHEAD)],
+                        n_in.at[last, m],
+                        no_send.at[last],
+                        n_last.at[m],
+                        {"win": o},
+                    )
+
+            to_all(give)
+
+    def last_finish():
+        for d in range(ulysses):
+            m = near_first(d)
+            arrived(n_in.at[last, m], n_last.at[m])
+            arrived(rl_in.at[m], r_last.at[m])
+            for f in range(FR):
+                pool[f, 0] = blended[m, f]
+            for f in range(AHEAD):
+                pool[FR + f, 0] = n_in[last, m, f]
+            for c in range(given):
+                pool[FR + AHEAD + c, 0] = rl_in[m, c]
+            at = columns(m, last)
+            for f in range(FR):
+                owned_ref[f, :, at] = pool[owned_at[f], 0]
+            for j in range(WF):
+                next_ref[j, :, at] = pool[next_at + j, 0]
+
     def step(i, carry):
         for lag, work in (
             (LAG_BLEND, blend),
@@ -369,25 +484,39 @@
             (LAG_LAST, finish),
         ):
 
-            @pl.when((i >= lag) & (i < steps + lag))
+            @pl.when((i >= lag) & (i < last + lag))
             def _(lag=lag, work=work):
                 work(i - lag)
 
         return carry
 
-    lax.fori_loop(0, steps + LAG_LAST, step, 0)
+    lax.fori_loop(0, last, step, 0)
+    blend(last - 1)
+    last_attention()
+    give_back(last - 1)
+    finish(last - 2)
+    last_blend()
+    finish(last - 1)
+    last_finish()
 
     def sent(s, carry):
         arrived(inbox.at[0, s, pl.ds(0, ulysses - 1)], q_send.at[s])
         arrived(inbox.at[1, s, pl.ds(0, ulysses - 1)], k_send.at[s])
         arrived(vbox.at[s, pl.ds(0, ulysses - 1)], v_send.at[s])
-        arrived(halo_in.at[s], ho_send.at[s])
         arrived(x_out.at[s, pl.ds(0, ulysses - 1)], xo_send.at[s])
         arrived(n_in.at[s], no_send.at[s])
         arrived(r_in.at[s], ro_send.at[s])
         return carry
 
     lax.fori_loop(0, steps, sent, 0)
+
+    def halo_sent(s, carry):
+        arrived(halo_in.at[s], ho_send.at[s])
+        return carry
+
+    lax.fori_loop(0, last, halo_sent, 0)
+    for u in range(ulysses):
+        arrived(raw_in.at[u, pl.ds(FR, 2 * HALO)], raw_send.at[u])
 
 
 def per_device(
@@ -439,6 +568,11 @@
             pltpu.VMEM((steps, given) + frame, bf16),
             pltpu.VMEM((steps, ulysses, AHEAD, local, head), bf16),
             pltpu.VMEM((FR + AHEAD + given,) + frame, bf16),
+            pltpu.VMEM((ulysses, WF, local, head), bf16),
+            pltpu.VMEM((ulysses, FR + 2 * HALO, local, head), bf16),
+            pltpu.VMEM((ulysses, FR, local, head), bf16),
+            pltpu.VMEM((ulysses, given, local, head), bf16),
+            pltpu.VMEM((ulysses, given, local, head), bf16),
             pltpu.SMEM((windows,), jnp.int32),
             pltpu.SMEM((FR,), jnp.int32),
             pltpu.SMEM((FR,), jnp.float32),
@@ -447,7 +581,9 @@
             pltpu.SMEM((windows * share,), jnp.int32),
             pltpu.SMEM((FR,), jnp.int32),
         ]
-        + [sems] * 14
+        + [sems, pltpu.SemaphoreType.DMA((steps, ulysses))]
+        + [sems] * 12
+        + [pltpu.SemaphoreType.DMA((ulysses,))] * 4
         + [pltpu.SemaphoreType.DMA((CHUNKS,))] * 2,
         compiler_params=pltpu.CompilerParams(
             collective_id=0, has_side_effects=True, vmem_limit_bytes=62 * 1000 * 1000

time: 139 us -> 137 us (0.986)
  no operation moved by 1% of the time
where the time goes in v2:
time: 137 us
  Pallas kernels  134 us (98%)
  local copies, waits for them, and re-layouts  2.77 us (2%)
    pallas_call x1, Pallas kernels, per_device(): pl.pallas_call(functools.partial(fused, (ulysses, windows, share, given,...  134 us
    unnamed x2, local copies, waits for them, and re-layouts  2.77 us

profile of v2, /device:TPU:0, one launch (start us, length us, event | category | flops | bytes accessed | tf_op | source)
XLA Modules:
  0.0 137.1 jit_solution(14993764119005658021)
XLA Ops:
  0.6 133.7 %shard_map.95 = (bf16[12,16,5120]{2,1,0:T(8,128)(2,1)S(1)}, bf16[16,16,5120]{2,1,0:T(8,128)(2,1)S(1)}) custom-call(s32[4]{0:T(128)} %start_ref.1, s32[4]{0:T(128)} %owner_ref.1, s32[4,16]{1,0:T(4,128)} %weight_ref.1, bf16[256,5120]{1,0:T(8,128)(2,1)} %bitcast.7, bf16[256,5120]{1,0:T(8,128)(2,1)} %bitcast.8, bf16[256,5120]{1,0:T(8,128)(2,1)} %bitcast.9, ...), custom_call_target="tpu_custom_call" | custom-call | tf_op jit(solution)/shard_map/pallas_call | solution.py:547
  134.3 1.3 copy.12
  135.6 1.5 %copy.13 = bf16[1,16,16,5120]{3,2,1,0:T(8,128)(2,1)} copy(bf16[1,16,16,5120]{3,2,1,0:T(8,128)(2,1)S(1)} %bitcast.6) | data formatting | bytes 5242880

commit v3 on v2

--- a/solution.py
+++ b/solution.py
@@ -29,8 +29,8 @@
     q_ref,
     k_ref,
     v_ref,
-    qg_ref,
-    kg_ref,
+    qg_hbm,
+    kg_hbm,
     owned_ref,
     next_ref,
     q_now,
@@ -80,6 +80,9 @@
     r_last,
     q_load,
     k_load,
+    qg_ref,
+    kg_ref,
+    gain_load,
 ):
     ulysses, windows, share, given, steps, head, tokens = dims
     local = tokens // WF
@@ -122,6 +125,13 @@
         pl.semaphore_signal(
             barrier, inc=1, device_id={"win": far(d)}, device_id_type=pl.DeviceIdType.MESH
         )
+
+    gains = (
+        pltpu.make_async_copy(qg_hbm, qg_ref, gain_load.at[0]),
+        pltpu.make_async_copy(kg_hbm, kg_ref, gain_load.at[1]),
+    )
+    for copy in gains:
+        copy.start()
 
     def remote(source, target, send, recv, to):
         pltpu.make_async_remote_copy(
@@ -250,6 +260,7 @@
             return carry
 
         lax.fori_loop(0, tokens // ROWS, norm_block, 0)
+        gains[which].wait()
         scale_columns(which, 0)
 
     pl.semaphore_wait(barrier, ulysses + windows - 2)
@@ -262,7 +273,7 @@
 
     next_at = tables()
 
-    scale = 1.0 / math.sqrt(head)
+    scale = 1.0 / math.sqrt(head) / math.log(2.0)
 
     def attend(s, then):
         keys = inbox[1, s].reshape(ulysses * tokens, head)
@@ -270,16 +281,13 @@
         for d in range(ulysses):
             u = near_first(d)
             arrived(inbox.at[0, s, u], q_recv.at[s, u])
-            scores = (
-                lax.dot_general(
-                    inbox[0, s, u],
-                    keys,
-                    (((1,), (1,)), ((), ())),
-                    preferred_element_type=jnp.float32,
-                )
-                * scale
+            scores = lax.dot_general(
+                inbox[0, s, u],
+                keys,
+                (((1,), (1,)), ((), ())),
+                preferred_element_type=jnp.float32,
             )
-            exponent = jnp.exp(scores - jnp.max(scores, axis=-1, keepdims=True))
+            exponent = jnp.exp2((scores - jnp.max(scores, axis=-1, keepdims=True)) * scale)
             inverse_sum = 1.0 / jnp.sum(exponent, axis=-1, keepdims=True)
             weights = (exponent * inverse_sum).astype(jnp.bfloat16)
             result = jnp.dot(weights, values, preferred_element_type=jnp.float32)
@@ -298,20 +306,20 @@
         send_scored(0, s + 1)
 
         def keep(u, result):
-            attended[s, :, u] = result
+            attended[s, u] = result
+
+            def send(side, at, to):
+                return lambda: remote(
+                    attended.at[s, u, pl.ds(at, HALO)],
+                    halo_in.at[s, u, pl.ds(side * HALO, HALO)],
+                    ho_send.at[s],
+                    ho_recv.at[s],
+                    {"win": to},
+                )
+
+            both_halos(send(1, 0, below), send(0, FR, above))
 
         attend(s, keep)
-
-        def send(side, at, to):
-            return lambda: remote(
-                attended.at[s, pl.ds(at, HALO)],
-                halo_in.at[s, side],
-                ho_send.at[s],
-                ho_recv.at[s],
-                {"win": to},
-            )
-
-        both_halos(send(1, 0, below), send(0, FR, above))
 
         @pl.when(s + 2 < steps)
         def _():
@@ -320,24 +328,24 @@
 
     def blend(s):
         arrived(halo_in.at[s], ho_recv.at[s])
-        for side in range(2):
-            halo_now[side * HALO : (side + 1) * HALO] = halo_in[s, side]
-        for f in range(FR):
-            numerator = near_w[f] * attended[s, near_at[f]].astype(jnp.float32)
-            denominator = near_w[f]
-            if f < HALO or f >= FR - HALO:
-                numerator += far_w[f] * halo_now[far_at[f]].astype(jnp.float32)
-                denominator += far_w[f]
-            x_out[s, :, f] = (numerator / denominator).astype(jnp.bfloat16)
-        spread(
-            lambda u: x_out.at[s, u],
-            lambda u: x_in.at[s, u],
-            xo_send.at[s],
-            xo_recv.at[s],
-        )
+        for d in range(ulysses):
+            u = near_first(ulysses - 1 - d)
+            for f in range(2 * HALO):
+                halo_now[f, 0] = halo_in[s, u, f]
+            for f in range(FR):
+                numerator = near_w[f] * attended[s, u, near_at[f]].astype(jnp.float32)
+                denominator = near_w[f]
+                if f < HALO or f >= FR - HALO:
+                    numerator += far_w[f] * halo_now[far_at[f], 0].astype(jnp.float32)
+                    denominator += far_w[f]
+                x_out[s, u, f] = (numerator / denominator).astype(jnp.bfloat16)
+            if d < ulysses - 1:
+                remote(x_out.at[s, u], x_in.at[s, me], xo_send.at[s], xo_recv.at[s], {"uly": u})
+            else:
+                pltpu.make_async_copy(x_out.at[s, u], x_in.at[s, me], xo_recv.at[s]).start()
 
     def to_all(give):
-        for d in range(1, windows):
+        for d in range(windows - 1, 0, -1):
 
             @pl.when(my_window + d < windows)
             def _(d=d):
@@ -494,8 +502,8 @@
     blend(last - 1)
     last_attention()
     give_back(last - 1)
+    last_blend()
     finish(last - 2)
-    last_blend()
     finish(last - 1)
     last_finish()
 
@@ -550,7 +558,7 @@
             pltpu.VMEM((FR, local, features), bf16),
             pltpu.VMEM((WF, local, features), bf16),
         ),
-        in_specs=[smem] * 3 + [hbm] * 3 + [vmem] * 2,
+        in_specs=[smem] * 3 + [hbm] * 5,
         out_specs=(vmem, vmem),
         scratch_shapes=[
             pltpu.VMEM((tokens, features), bf16),
@@ -559,8 +567,8 @@
             pltpu.VMEM((2, ulysses, steps, tokens, head), bf16),
             pltpu.VMEM((2, steps, ulysses, tokens, head), bf16),
             pltpu.VMEM((steps, ulysses, tokens, head), bf16),
-            pltpu.VMEM((steps, WF) + frame, bf16),
-            pltpu.VMEM((steps, 2, HALO) + frame, bf16),
+            pltpu.VMEM((steps, ulysses, WF, local, head), bf16),
+            pltpu.VMEM((steps, ulysses, 2 * HALO, local, head), bf16),
             pltpu.VMEM((2 * HALO,) + frame, bf16),
             pltpu.VMEM((steps, ulysses, FR, local, head), bf16),
             pltpu.VMEM((steps, ulysses, FR, local, head), bf16),
@@ -584,7 +592,9 @@
         + [sems, pltpu.SemaphoreType.DMA((steps, ulysses))]
         + [sems] * 12
         + [pltpu.SemaphoreType.DMA((ulysses,))] * 4
-        + [pltpu.SemaphoreType.DMA((CHUNKS,))] * 2,
+        + [pltpu.SemaphoreType.DMA((CHUNKS,))] * 2
+        + [pltpu.VMEM((1, features), jnp.float32)] * 2
+        + [pltpu.SemaphoreType.DMA((2,))],
         compiler_params=pltpu.CompilerParams(
             collective_id=0, has_side_effects=True, vmem_limit_bytes=62 * 1000 * 1000
         ),

time: 137 us -> 136 us (level)
  Pallas kernels: 134 us -> 132 us
    pallas_call x1, Pallas kernels: 134 us -> 132 us  [per_device(): pl.pallas_call(functools.partial(fused, (ulysses, windows, share, given,...]
where the time goes in v3:
time: 136 us
  Pallas kernels  132 us (97%)
  local copies, waits for them, and re-layouts  2.77 us (2%)
    pallas_call x1, Pallas kernels, per_device(): pl.pallas_call(functools.partial(fused, (ulysses, windows, share, given,...  132 us
    unnamed x2, local copies, waits for them, and re-layouts  2.77 us

profile of v3, /device:TPU:0, one launch (start us, length us, event | category | flops | bytes accessed | tf_op | source)
XLA Modules:
  0.0 135.7 jit_solution(13106797412606845673)
XLA Ops:
  0.6 132.3 %shard_map.95 = (bf16[12,16,5120]{2,1,0:T(8,128)(2,1)S(1)}, bf16[16,16,5120]{2,1,0:T(8,128)(2,1)S(1)}) custom-call(s32[4]{0:T(128)} %start_ref.1, s32[4]{0:T(128)} %owner_ref.1, s32[4,16]{1,0:T(4,128)} %weight_ref.1, bf16[256,5120]{1,0:T(8,128)(2,1)} %bitcast.7, bf16[256,5120]{1,0:T(8,128)(2,1)} %bitcast.8, bf16[256,5120]{1,0:T(8,128)(2,1)} %bitcast.9, ...), custom_call_target="tpu_custom_call" | custom-call | tf_op jit(solution)/shard_map/pallas_call | solution.py:555
  132.9 1.3 copy.12
  134.2 1.5 %copy.13 = bf16[1,16,16,5120]{3,2,1,0:T(8,128)(2,1)} copy(bf16[1,16,16,5120]{3,2,1,0:T(8,128)(2,1)S(1)} %bitcast.6) | data formatting | bytes 5242880

commit v4 on v3

--- a/solution.py
+++ b/solution.py
@@ -17,7 +17,7 @@
 CHUNKS = 4
 LAG_BLEND = 1
 LAG_RETURN = 1
-LAG_LAST = 2
+LAG_LAST = 3
 ROWS = 16
 
 
@@ -321,11 +321,6 @@
 
         attend(s, keep)
 
-        @pl.when(s + 2 < steps)
-        def _():
-            for which in range(2):
-                scale_columns(which, s + 2)
-
     def blend(s):
         arrived(halo_in.at[s], ho_recv.at[s])
         for d in range(ulysses):
@@ -496,12 +491,18 @@
             def _(lag=lag, work=work):
                 work(i - lag)
 
+        @pl.when(i + 2 < steps)
+        def _():
+            for which in range(2):
+                scale_columns(which, i + 2)
+
         return carry
 
     lax.fori_loop(0, last, step, 0)
     blend(last - 1)
     last_attention()
     give_back(last - 1)
+    finish(last - 3)
     last_blend()
     finish(last - 2)
     finish(last - 1)

time: 136 us -> 136 us (level)
  no operation moved by 1% of the time
where the time goes in v4:
time: 136 us
  Pallas kernels  132 us (97%)
  local copies, waits for them, and re-layouts  2.77 us (2%)
    pallas_call x1, Pallas kernels, per_device(): pl.pallas_call(functools.partial(fused, (ulysses, windows, share, given,...  132 us
    unnamed x2, local copies, waits for them, and re-layouts  2.77 us

profile of v4, /device:TPU:0, one launch (start us, length us, event | category | flops | bytes accessed | tf_op | source)
XLA Modules:
  0.0 135.7 jit_solution(11534337570007416380)
XLA Ops:
  0.6 132.3 %shard_map.95 = (bf16[12,16,5120]{2,1,0:T(8,128)(2,1)S(1)}, bf16[16,16,5120]{2,1,0:T(8,128)(2,1)S(1)}) custom-call(s32[4]{0:T(128)} %start_ref.1, s32[4]{0:T(128)} %owner_ref.1, s32[4,16]{1,0:T(4,128)} %weight_ref.1, bf16[256,5120]{1,0:T(8,128)(2,1)} %bitcast.7, bf16[256,5120]{1,0:T(8,128)(2,1)} %bitcast.8, bf16[256,5120]{1,0:T(8,128)(2,1)} %bitcast.9, ...), custom_call_target="tpu_custom_call" | custom-call | tf_op jit(solution)/shard_map/pallas_call | solution.py:556
  132.9 1.3 copy.12
  134.2 1.5 %copy.13 = bf16[1,16,16,5120]{3,2,1,0:T(8,128)(2,1)} copy(bf16[1,16,16,5120]{3,2,1,0:T(8,128)(2,1)S(1)} %bitcast.6) | data formatting | bytes 5242880
